TPU v7x, 128 devices: a whole 4x4x4 slice. The times are simulated.
128 devices in a mesh: req: 8 (over x, core), exp: 16 (over y, z).
Axes of the slice: x: 4, y: 4, z: 4, core: 2. Of those that a mesh axis runs over, the one named last changes fastest.
Arguments:
- queries: bfloat16 [8192, 2048], P('req', 'exp'), may hold values from -6 to 6
- keys: bfloat16 [8192, 2048], P('req', 'exp'), may hold values from -15 to 15
- values: bfloat16 [8192, 2048], P('req', 'exp'), may hold values from -6 to 6
- prefix_keys: bfloat16 [4, 4096, 2048], P(None, 'req', 'exp'), may hold values from -15 to 15
- prefix_values: bfloat16 [4, 4096, 2048], P(None, 'req', 'exp'), may hold values from -6 to 6
- lengths: int32 [8, 8], P('req'), may hold values from 1 to 512, 1024 in all within a row
- groups: int32 [8, 8], P('req'), may hold values from 0 to 3
- residual: bfloat16 [8192, 2048], P(('req', 'exp')), may hold values from -6 to 6
- out_proj: bfloat16 [2048, 2048], P('exp'), may hold values from -0.125 to 0.125
- norm_gain: bfloat16 [2048], replicated, may hold values from 0.099609375 to 1.8984375
- expert_ids: int32 [8192, 4], P(('req', 'exp')), may hold values from 0 to 31, all different within a row; in each aligned block of 64 rows (0 to 63, 64 to 127, ...) at most 16 rows name the same one
- expert_gates: bfloat16 [8192, 4], P(('req', 'exp')), may hold values from 0.049804688 to 0.5
- w_gate: bfloat16 [32, 2048, 704], P('exp'), may hold values from -0.125 to 0.125
- w_up: bfloat16 [32, 2048, 704], P('exp'), may hold values from -0.125 to 0.125
- w_down: bfloat16 [32, 704, 2048], P('exp'), may hold values from -0.21875 to 0.21875
Outputs:
- layer_out: bfloat16 [8192, 2048], P(('req', 'exp'))
Inputs may be any that keep to these rules, and one draw needn't show every extreme that they name: The 8 lengths of a row sum to 1024; the longest request of each row has half of 1024 tokens. `expert_ids`: each row names 4 different experts. Among the 64 tokens of one device, no expert is named more than 16 times; on some device some expert is named exactly 16 times.
All inputs are finite; a program needn't handle non-finite values.
Results may differ from a plain program's by a relative error of at most 0.02.
Values may be sent and summed in bfloat16 or wider, within the bound.
A program may use at most 256 MiB of HBM per device.

v0:
```python
import math
import jax
import jax.numpy as jnp
from jax import lax
from jax.sharding import PartitionSpec as P

HEAD = 128
TOPK = 4
EXPERTS = 32
G = 4
RQ = 8
ROW_TOK = 1024
NEG = -1e30


def token_layout(lengths, groups):
    req_ends = jnp.cumsum(lengths, axis=-1)
    starts = req_ends - lengths
    position = jnp.arange(ROW_TOK, dtype=jnp.int32)
    request = jnp.sum((position[None, :, None] >= req_ends[:, None, :]).astype(jnp.int32), axis=-1)
    onehot = request[:, :, None] == jnp.arange(RQ, dtype=jnp.int32)[None, None, :]
    first_tok = jnp.sum(jnp.where(onehot, starts[:, None, :], 0), axis=-1)
    tok_group = jnp.sum(jnp.where(onehot, groups[:, None, :], 0), axis=-1)
    return (request, position[None, :] - first_tok, tok_group)


def split_blocks(row_count):
    if row_count % 1024 == 0 and row_count > 1024:
        return row_count // 1024
    return 1


def pack_parts(parts):
    return jnp.concatenate([parts[0], parts[1], parts[2]], axis=1)


def unpack_parts(packed, head_count):
    columns = head_count * HEAD
    return (
        packed[:, :columns],
        packed[:, columns : columns + head_count],
        packed[:, columns + head_count :],
    )


def attend_prefix(query_rows, query_group, prefix_k, prefix_v):
    row_count, columns = query_rows.shape
    head_count = columns // HEAD
    span = prefix_k.shape[1]
    key_grid = prefix_k.reshape(G, span, head_count, HEAD)
    val_grid = prefix_v.reshape(G, span, head_count, HEAD)
    blocks = split_blocks(row_count)
    block_len = row_count // blocks
    scaling = 1.0 / math.sqrt(HEAD)

    def per_block(pieces):
        block_q, block_g = pieces
        query_grid = block_q.reshape(block_len, head_count, HEAD)
        scores = (
            jnp.einsum("qhd,gkhd->hqgk", query_grid, key_grid, preferred_element_type=jnp.float32)
            * scaling
        )
        member = block_g[:, None] == jnp.arange(G, dtype=jnp.int32)[None, :]
        scores = jnp.where(member[None, :, :, None], scores, NEG)
        maxima = jnp.max(scores, axis=(2, 3))
        exp_terms = jnp.exp(scores - maxima[:, :, None, None])
        totals = jnp.sum(exp_terms, axis=(2, 3))
        weighted = jnp.einsum(
            "hqgk,gkhd->qhd",
            exp_terms.astype(jnp.bfloat16),
            val_grid,
            preferred_element_type=jnp.float32,
        )
        return (weighted.reshape(block_len, columns), maxima.T, totals.T)

    weighted, maxima, totals = lax.map(
        per_block,
        (query_rows.reshape(blocks, block_len, columns), query_group.reshape(blocks, block_len)),
    )
    return (
        weighted.reshape(row_count, columns),
        maxima.reshape(row_count, head_count),
        totals.reshape(row_count, head_count),
    )


def attend_suffix(queries, keys, values, request, position):
    row_count, columns = queries.shape
    head_count = columns // HEAD
    blocks = split_blocks(row_count)
    block_len = row_count // blocks
    scaling = 1.0 / math.sqrt(HEAD)
    key_grid = keys.reshape(row_count, head_count, HEAD)
    val_grid = values.reshape(row_count, head_count, HEAD)

    def per_block(pieces):
        block_q, block_req, block_pos = pieces
        query_grid = block_q.reshape(block_len, head_count, HEAD)
        scores = (
            jnp.einsum("qhd,khd->hqk", query_grid, key_grid, preferred_element_type=jnp.float32)
            * scaling
        )
        allowed = (request[None, :] == block_req[:, None]) & (
            position[None, :] <= block_pos[:, None]
        )
        scores = jnp.where(allowed[None, :, :], scores, NEG)
        maxima = jnp.max(scores, axis=2)
        exp_terms = jnp.exp(scores - maxima[:, :, None])
        totals = jnp.sum(exp_terms, axis=2)
        weighted = jnp.einsum(
            "hqk,khd->qhd",
            exp_terms.astype(jnp.bfloat16),
            val_grid,
            preferred_element_type=jnp.float32,
        )
        return (weighted.reshape(block_len, columns), maxima.T, totals.T)

    weighted, maxima, totals = lax.map(
        per_block,
        (
            queries.reshape(blocks, block_len, columns),
            request.reshape(blocks, block_len),
            position.reshape(blocks, block_len),
        ),
    )
    return (
        weighted.reshape(row_count, columns),
        maxima.reshape(row_count, head_count),
        totals.reshape(row_count, head_count),
    )


def combine(former, latter):
    weighted_a, maxima_a, totals_a = former
    weighted_b, maxima_b, totals_b = latter
    row_count, head_count = maxima_a.shape
    maxima = jnp.maximum(maxima_a, maxima_b)
    factor_a = jnp.exp(maxima_a - maxima)
    factor_b = jnp.exp(maxima_b - maxima)
    weighted = (
        weighted_a.reshape(row_count, head_count, HEAD) * factor_a[:, :, None]
        + weighted_b.reshape(row_count, head_count, HEAD) * factor_b[:, :, None]
    )
    return (
        weighted.reshape(row_count, head_count * HEAD),
        maxima,
        totals_a * factor_a + totals_b * factor_b,
    )


def per_device(
    queries,
    keys,
    values,
    prefix_keys,
    prefix_values,
    lengths,
    groups,
    residual,
    out_proj,
    norm_gain,
    expert_ids,
    expert_gates,
    w_gate,
    w_up,
    w_down,
):
    row_tok, columns = queries.shape
    head_count = columns // HEAD
    tok_dev = residual.shape[0]
    request, position, tok_group = token_layout(lengths, groups)
    request, position, tok_group = (request[0], position[0], tok_group[0])
    all_groups = lax.all_gather(tok_group, "req", axis=0, tiled=True)
    partial_value = pack_parts(
        attend_prefix(
            lax.all_gather(queries, "req", axis=0, tiled=True),
            all_groups,
            prefix_keys,
            prefix_values,
        )
    )
    returned = lax.all_to_all(partial_value, "req", split_axis=0, concat_axis=0, tiled=True)
    owners = returned.shape[0] // row_tok
    back_w, back_m, back_t = unpack_parts(returned, head_count)
    all_weighted = back_w.reshape(owners, row_tok, head_count, HEAD)
    all_maxima = back_m.reshape(owners, row_tok, head_count)
    all_totals = back_t.reshape(owners, row_tok, head_count)
    maxima = jnp.max(all_maxima, axis=0)
    factor = jnp.exp(all_maxima - maxima[None])
    weighted = jnp.sum(all_weighted * factor[..., None], axis=0).reshape(row_tok, columns)
    prefix_part = (weighted, maxima, jnp.sum(all_totals * factor, axis=0))
    suffix_part = attend_suffix(queries, keys, values, request, position)
    weighted, maxima, totals = combine(prefix_part, suffix_part)
    attended = (
        (weighted.reshape(row_tok, head_count, HEAD) / totals[:, :, None])
        .reshape(row_tok, columns)
        .astype(jnp.bfloat16)
    )
    exp_count = lax.axis_size("exp")
    full_proj = lax.all_gather(out_proj, "exp", axis=0, tiled=True)
    token_rows = lax.all_to_all(attended, "exp", split_axis=0, concat_axis=1, tiled=True)
    projected = jnp.dot(token_rows, full_proj, preferred_element_type=jnp.float32)
    stream = residual.astype(jnp.float32) + projected
    meansq = jnp.mean(stream * stream, axis=-1, keepdims=True)
    normed = (stream * lax.rsqrt(meansq + 1e-06) * norm_gain.astype(jnp.float32)).astype(
        jnp.bfloat16
    )
    capacity = max(2, tok_dev // 4)
    slot_count = EXPERTS * capacity
    flat_ids = expert_ids.reshape(-1)
    onehot = (flat_ids[:, None] == jnp.arange(EXPERTS, dtype=jnp.int32)[None, :]).astype(jnp.int32)
    slot_of = jnp.sum(onehot * (jnp.cumsum(onehot, axis=0) - 1), axis=1)
    dest = flat_ids * capacity + slot_of
    dest_hot = dest[:, None] == jnp.arange(slot_count, dtype=jnp.int32)[None, :]
    select = jnp.sum(dest_hot.reshape(tok_dev, TOPK, slot_count).astype(jnp.float32), axis=1)
    buffer = (
        jnp.dot(select.T.astype(jnp.bfloat16), normed, preferred_element_type=jnp.float32)
        .astype(jnp.bfloat16)
        .reshape(EXPERTS, capacity, normed.shape[1])
    )
    exp_dev = w_gate.shape[0]
    received = lax.all_to_all(buffer, "exp", split_axis=0, concat_axis=0, tiled=True)
    slots = received.shape[1]
    grid_in = received.reshape(exp_count, exp_dev, slots, received.shape[2])
    gate_h = jnp.einsum("secd,edf->secf", grid_in, w_gate, preferred_element_type=jnp.float32)
    up_h = jnp.einsum("secd,edf->secf", grid_in, w_up, preferred_element_type=jnp.float32)
    hidden = (jax.nn.silu(gate_h) * up_h).astype(jnp.bfloat16)
    expert_out = jnp.einsum("secf,efd->secd", hidden, w_down, preferred_element_type=jnp.float32)
    returned = lax.all_to_all(
        expert_out.astype(jnp.bfloat16).reshape(EXPERTS, slots, received.shape[2]),
        "exp",
        split_axis=0,
        concat_axis=0,
        tiled=True,
    )
    gates = expert_gates.astype(jnp.float32).reshape(tok_dev, TOPK, 1)
    weights = jnp.sum(
        dest_hot.reshape(tok_dev, TOPK, slot_count).astype(jnp.float32) * gates, axis=1
    )
    mixture = jnp.dot(
        weights.astype(jnp.bfloat16),
        returned.reshape(slot_count, received.shape[2]),
        preferred_element_type=jnp.float32,
    )
    return (stream + mixture).astype(jnp.bfloat16)


def solution(mesh):
    in_specs = (
        P("req", "exp"),
        P("req", "exp"),
        P("req", "exp"),
        P(None, "req", "exp"),
        P(None, "req", "exp"),
        P("req", None),
        P("req", None),
        P(("req", "exp"), None),
        P("exp", None),
        P(),
        P(("req", "exp"), None),
        P(("req", "exp"), None),
        P("exp", None, None),
        P("exp", None, None),
        P("exp", None, None),
    )
    out_specs = P(("req", "exp"), None)
    return jax.shard_map(
        per_device, mesh=mesh, in_specs=in_specs, out_specs=out_specs, check_vma=False
    )
```

profile of v0, /device:TPU:0, one launch (start us, length us, event | category | flops | bytes accessed | tf_op | source)
XLA Modules:
  0.0 288.0 jit_solution(15104359768345971016)
XLA Ops:
  10.4 13.3 %all_gather.9 = s32[8192]{0:T(1024)S(1)} all-gather(s32[1024]{0:T(1024)S(1)} %get-tuple-element.81), channel_id=1, replica_groups=mesh['req'=8,'exp'=16] {'req'}, dimensions={0}, use_global_device_ids=true | all-gather | bytes 36864 | tf_op jit(solution)/shard_map/all_gather | solution.py:173
  23.6 13.1 %all-gather.3.cloned.1.call-done = bf16[8192,128]{1,0:T(8,128)(2,1)} async-done(((bf16[1024,128]{1,0:T(8,128)(2,1)}), bf16[8192,128]{1,0:T(8,128)(2,1)}) %all-gather.3.cloned.1.call-update) | async-done | bytes 2097168 | tf_op jit(solution)/shard_map/all_gather | solution.py:176
  36.7 55.3 %while.2 = (s32[]{:T(128)}, f32[8,1024,128]{1,2,0:T(8,128)}, f32[8,1024,1]{1,2,0:T(1,128)S(1)}, f32[8,1024,1]{1,2,0:T(1,128)S(1)}, s32[8,1024]{1,0:T(8,128)S(1)}...) while((s32[]{:T(128)}, f32[8,1024,128]{1,2,0:T(8,128)}, ...), condition=%wide.region_6.7_spmd, body=%wide.region_3.6_spmd.sunk | while | flops 1096812544 | bytes 29160576 | solution.py:76
  36.7 2.4 fusion.102
  40.9 2.8 fusion.103
  43.6 2.4 fusion.102
  47.8 2.7 fusion.103
  50.5 2.4 fusion.102
  54.7 2.7 fusion.103
  61.6 2.7 fusion.103
  64.3 2.4 fusion.102
  68.5 2.7 fusion.103
  75.4 2.8 fusion.103
  78.2 2.4 fusion.102
  82.3 2.8 fusion.103
  85.1 2.4 fusion.102
  89.2 2.8 fusion.103
  92.0 4.9 %pad_maximum_fusion = f32[8,1024,130]{1,2,0:T(8,128)} fusion(f32[8,1024,1]{1,2,0:T(1,128)S(1)} %get-tuple-element.78, f32[8,1024,1]{1,2,0:T(1,128)S(1)} %get-tuple-element.77, f32[8,1024,128]{1,2,0:T(8,128)} %get-tuple-element.76), kind=kLoop, calls=%fused_computation.27 | loop fusion | flops 2129920 | bytes 8519680 | tf_op jit(solution)/shard_map/concatenate | solution.py:34
  97.0 4.8 %all-to-all-start = ((f32[8,1024,130]{1,2,0:T(8,128)}), f32[8,1024,130]{1,2,0:T(8,128)}, u32[]{:S(2)}, u32[]{:S(2)}) async-start(f32[8,1024,130]{1,2,0:T(8,128)} %pad_maximum_fusion), calls=%async_computation | async-start | bytes 8912896 | tf_op jit(solution)/shard_map/all_to_all | solution.py:182
  107.1 47.1 %all-to-all-done = f32[8,1024,130]{1,2,0:T(8,128)} async-done(((f32[8,1024,130]{1,2,0:T(8,128)}), f32[8,1024,130]{1,2,0:T(8,128)}, u32[]{:S(2)}, u32[]{:S(2)}) %all-to-all-start) | async-done | bytes 4259872 | tf_op jit(solution)/shard_map/all_to_all | solution.py:182
  154.2 4.7 %copy.132 = f32[8,1024,130]{1,0,2:T(8,128)S(1)} copy(f32[8,1024,130]{1,2,0:T(8,128)} %all-to-all-done) | data formatting | bytes 8519680 | tf_op jit(solution)/shard_map/all_to_all | solution.py:182
  159.3 3.9 %copy.114 = f32[17,8,8,1024]{3,1,2,0:T(8,128)S(1)} copy(f32[17,8,8,1024]{3,2,1,0:T(8,128)S(1)} %bitcast.177) | data formatting | bytes 8912896
  165.8 7.9 %copy.115 = f32[16,8,8,1024]{3,2,1,0:T(8,128)} copy(f32[16,8,8,1024]{3,1,2,0:T(8,128)} %bitcast.181) | data formatting | bytes 8388608
  173.7 3.7 %fusion.26 = f32[1024,128]{0,1:T(8,128)S(1)} fusion(f32[16,8,8,1024]{3,2,1,0:T(8,128)} %copy.115, f32[8,1024]{1,0:T(8,128)S(1)} %subtract_exponential_fusion.2), kind=kLoop, calls=%fused_computation.30 | loop fusion | flops 1966080 | bytes 4751360 | tf_op jit(solution)/shard_map/reduce_sum | solution.py:190
  177.7 3.9 %fusion.68 = bf16[1024,1,128]{2,0,1:T(8,128)(2,1)} fusion(bf16[1024,128]{1,0:T(8,128)(2,1)S(1)} %copy-done.8, f32[1024,1024]{0,1:T(8,128)} %copy-done.1, f32[1024]{0:T(1024)S(1)} %get-tuple-element.109, f32[1024,128]{1,0:T(8,128)S(1)} %copy.91, f32[1024]{0:T(1024)S(1)} %get-tuple-element.101, f32[1024]{0:T(1024)S(1)} %get-tuple-element.103, ...), kind=kOutput, calls=%fused_computation.57 | convolution fusion | flops 271187968 | bytes 5259264 | tf_op jit(solution)/shard_map/while/body/eval_jaxpr/hqk,khd->qhd/dot_general | solution.py:110
  181.7 7.1 %all-to-all-start.1 = ((bf16[16,64,128]{2,1,0:T(8,128)(2,1)}), bf16[16,64,128]{2,1,0:T(8,128)(2,1)S(1)}, u32[]{:S(2)}, u32[]{:S(2)}) async-start(bf16[16,64,128]{2,1,0:T(8,128)(2,1)} %bitcast.22), calls=%async_computation.1 | async-start | bytes 524288 | tf_op jit(solution)/shard_map/all_to_all | solution.py:201
  188.9 8.3 %all-to-all-done.1 = bf16[16,64,128]{2,1,0:T(8,128)(2,1)S(1)} async-done(((bf16[16,64,128]{2,1,0:T(8,128)(2,1)}), bf16[16,64,128]{2,1,0:T(8,128)(2,1)S(1)}, u32[]{:S(2)}, u32[]{:S(2)}) %all-to-all-start.1) | async-done | bytes 262176 | tf_op jit(solution)/shard_map/all_to_all | solution.py:201
  197.2 5.1 %multiply_reduce_fusion = (f32[64]{0:T(128)S(1)}, f32[64,2048]{1,0:T(8,128)S(1)}) fusion(bf16[2048,2048]{1,0:T(8,128)(2,1)} %all-gather.5.cloned.1.call-done, bf16[64,2048]{1,0:T(8,128)(2,1)S(1)} %copy-done.2, bf16[16,64,128]{2,1,0:T(8,128)(2,1)S(1)} %all-to-all-done.1), kind=kOutput, calls=%fused_computation.61 | convolution fusion | flops 537395136 | bytes 9437440 | tf_op jit(solution)/shard_map/dot_general | solution.py:202
  203.1 30.3 %all_to_all.35 = bf16[32,16,2048]{2,1,0:T(8,128)(2,1)S(1)} all-to-all(bf16[32,16,2048]{2,1,0:T(8,128)(2,1)S(1)} %bitcast.183), channel_id=1, replica_groups=mesh['req'=8,'exp'=16] {'exp'}, dimensions={0} | all-to-all | bytes 4194304 | tf_op jit(solution)/shard_map/all_to_all | solution.py:222
  233.4 5.6 %fusion.24 = f32[2,16,16,704]{3,2,1,0:T(8,128)} fusion(bf16[2,2048,704]{1,2,0:T(8,128)(2,1)} %param.29, bf16[16,2,16,2048]{3,2,1,0:T(8,128)(2,1)S(1)} %bitcast.185), kind=kOutput, calls=%fused_computation.25 | convolution fusion | flops 1476395008 | bytes 9306112 | tf_op jit(solution)/shard_map/secd,edf->secf/dot_general | solution.py:225
  239.0 9.7 %fusion.32 = bf16[16,2,16,2048]{3,2,0,1:T(8,128)(2,1)} fusion(bf16[2,704,2048]{2,1,0:T(8,128)(2,1)} %param.31, f32[2,16,16,704]{3,2,1,0:T(8,128)} %fusion.24, bf16[2,2048,704]{1,2,0:T(8,128)(2,1)} %param.30, bf16[16,2,16,2048]{3,2,1,0:T(8,128)(2,1)S(1)} %bitcast.186), kind=kOutput, calls=%fused_computation.37 | convolution fusion | flops 2956001280 | bytes 17170432 | tf_op jit(solution)/shard_map/secf,efd->secd/dot_general | solution.py:228
  250.5 29.5 %all_to_all.36 = bf16[32,16,2048]{2,1,0:T(8,128)(2,1)S(1)} all-to-all(bf16[32,16,2048]{2,1,0:T(8,128)(2,1)S(1)} %bitcast.184), channel_id=1, replica_groups=mesh['req'=8,'exp'=16] {'exp'}, dimensions={0} | all-to-all | bytes 4194304 | tf_op jit(solution)/shard_map/all_to_all | solution.py:229
  (112 shorter events, 34.8 us)
Async XLA Ops:
  6.5 96.9 %copy-start = (bf16[1024,128]{1,0:T(8,128)(2,1)S(1)}, bf16[1024,128]{1,0:T(8,128)(2,1)}, u32[]{:S(2)}) copy-start(bf16[1024,128]{1,0:T(8,128)(2,1)} %param.18) | copy-start | bytes 786436
  6.5 30.2 %all-gather.3.cloned.1.call-start = ((), (), s32[]{:S(2)}) async-start(), calls=%async_computation.4 | async-start | bytes 2359296 | tf_op jit(solution)/shard_map/all_gather | solution.py:176
  7.3 190.0 %all-gather.5.cloned.1.call-start = ((), (), s32[]{:S(2)}) async-start(), calls=%async_computation.5 | async-start | bytes 8912896 | tf_op jit(solution)/shard_map/all_gather | solution.py:200
  39.1 1.7 copy-start.7
  46.0 1.7 copy-start.7
  52.9 1.7 copy-start.7
  59.8 1.7 copy-start.7
  66.7 1.7 copy-start.7
  73.6 1.7 copy-start.7
  80.5 1.7 copy-start.7
  87.5 1.7 copy-start.7
  97.0 4.8 %copy-start.4 = (s32[64,4]{0,1:T(4,128)S(1)}, s32[64,4]{0,1:T(4,128)}, u32[]{:S(2)}) copy-start(s32[64,4]{0,1:T(4,128)} %param.27) | copy-start | bytes 3076
  97.0 6.4 %copy-start.6 = (bf16[64,4]{0,1:T(4,128)(2,1)S(1)}, bf16[64,4]{0,1:T(4,128)(2,1)}, u32[]{:S(2)}) copy-start(bf16[64,4]{0,1:T(4,128)(2,1)} %param.28) | copy-start | bytes 1540
  97.0 6.4 %copy-start.5 = (bf16[2048]{0:T(1024)(128)(2,1)S(1)}, bf16[2048]{0:T(1024)(128)(2,1)}, u32[]{:S(2)}) copy-start(bf16[2048]{0:T(1024)(128)(2,1)} %param.26) | copy-start | bytes 12292
  97.0 6.5 %copy-start.3 = (bf16[1024,128]{1,0:T(8,128)(2,1)S(1)}, bf16[1024,128]{1,0:T(8,128)(2,1)}, u32[]{:S(2)}) copy-start(bf16[1024,128]{1,0:T(8,128)(2,1)} %param.17) | copy-start | bytes 786436
  97.0 57.3 %all-to-all-start = ((f32[8,1024,130]{1,2,0:T(8,128)}), f32[8,1024,130]{1,2,0:T(8,128)}, u32[]{:S(2)}, u32[]{:S(2)}) async-start(f32[8,1024,130]{1,2,0:T(8,128)} %pad_maximum_fusion), calls=%async_computation | async-start | bytes 8912896 | tf_op jit(solution)/shard_map/all_to_all | solution.py:182
  104.5 2.0 copy-start.1
  173.7 4.0 %copy-start.8 = (bf16[1024,128]{1,0:T(8,128)(2,1)S(1)}, bf16[1024,128]{1,0:T(8,128)(2,1)}, u32[]{:S(2)}) copy-start(bf16[1024,128]{1,0:T(8,128)(2,1)} %param.19) | copy-start | bytes 786436
  177.4 19.8 %copy-start.2 = (bf16[64,2048]{1,0:T(8,128)(2,1)S(1)}, bf16[64,2048]{1,0:T(8,128)(2,1)}, u32[]{:S(2)}) copy-start(bf16[64,2048]{1,0:T(8,128)(2,1)} %param.24) | copy-start | bytes 786436
  181.7 15.6 %all-to-all-start.1 = ((bf16[16,64,128]{2,1,0:T(8,128)(2,1)}), bf16[16,64,128]{2,1,0:T(8,128)(2,1)S(1)}, u32[]{:S(2)}, u32[]{:S(2)}) async-start(bf16[16,64,128]{2,1,0:T(8,128)(2,1)} %bitcast.22), calls=%async_computation.1 | async-start | bytes 524288 | tf_op jit(solution)/shard_map/all_to_all | solution.py:201
Sparse Core Ops, SparseCore 0:
  9.1 27.5 all-gather.2
  38.8 71.1 all-gather.4
where the time goes:
time: 289 us; the launch traced here: 288 us
  blocking collectives  73 us (25%)
  waiting for transfers between devices  69.9 us (24%)
  matrix products  68.5 us (24%)
  other arithmetic  26.5 us (9%)
  local copies, waits for them, and re-layouts  24.2 us (8%)
  between operations  13.7 us (5%)
  starting transfers between devices  11.9 us (4%)
    all_to_all x1, waiting for transfers between devices, per_device(): lax.all_to_all(partial_value, 'req', split_axis=0, concat_axis=0, tiled=T...  47.1 us
    all_to_all x1, blocking collectives, per_device(): lax.all_to_all(buffer, 'exp', split_axis=0, concat_axis=0, tiled=True)  30.3 us
    all_to_all x1, blocking collectives, per_device(): lax.all_to_all(expert_out.astype(jnp.bfloat16).reshape(EXPERTS, slots, re...  29.5 us
    dot_general x8, matrix products, per_block(): jnp.einsum('hqgk,gkhd->qhd', exp_terms.astype(jnp.bfloat16), val_grid, pr...  22 us
    dot_general x8, matrix products, per_block(): jnp.einsum('qhd,gkhd->hqgk', query_grid, key_grid, preferred_element_type...  19.1 us
    unnamed x20, local copies, waits for them, and re-layouts  14.2 us
    reduce_sum x8, other arithmetic, per_block(): totals = jnp.sum(exp_terms, axis=(2, 3))  13.7 us
    all_gather x1, blocking collectives, per_device(): all_groups = lax.all_gather(tok_group, 'req', axis=0, tiled=True)  13.3 us
  transfers between devices with their start and end apart: 4, of which 3 were waited for; matrix products, arithmetic and copies ran while one was open for 32% of the time, Pallas kernels for 0%

commit v1 on v0

--- a/solution.py
+++ b/solution.py
@@ -170,7 +170,9 @@
     tok_dev = residual.shape[0]
     request, position, tok_group = token_layout(lengths, groups)
     request, position, tok_group = (request[0], position[0], tok_group[0])
-    all_groups = lax.all_gather(tok_group, "req", axis=0, tiled=True)
+    all_groups = jnp.concatenate(
+        lax.all_to_all(jnp.stack([tok_group] * lax.axis_size("req")), "req", 0, 0), axis=0
+    )
     partial_value = pack_parts(
         attend_prefix(
             lax.all_gather(queries, "req", axis=0, tiled=True),

time: 289 us -> 289 us (level)
  blocking collectives: 73 us -> 59.8 us
  waiting for transfers between devices: 69.9 us -> 78.2 us
  starting transfers between devices: 11.9 us -> 16.3 us
    all_gather x1 -> x0, blocking collectives: 13.3 us -> none  [per_device(): all_groups = lax.all_gather(tok_group, 'req', axis=0, tiled=True)]
    all_to_all x0 -> x1, waiting for transfers between devices: none -> 4.67 us  [per_device(): lax.all_to_all(jnp.stack([tok_group] * lax.axis_size('req')), 'req', 0, 0)]
    all_to_all x0 -> x1, starting transfers between devices: none -> 4.38 us  [per_device(): lax.all_to_all(jnp.stack([tok_group] * lax.axis_size('req')), 'req', 0, 0)]
    all_gather x1, waiting for transfers between devices: 13.1 us -> 16.6 us  [per_device(): lax.all_gather(queries, 'req', axis=0, tiled=True)]
    unnamed x20 -> x21, local copies, waits for them, and re-layouts: 14.2 us -> 14.2 us
  transfers between devices with their start and end apart: 4 -> 5, of which waited for: 3 -> 4; matrix products, arithmetic and copies ran while one was open for 32% -> 33% of each run, Pallas kernels for 0% -> 0%
where the time goes in v1:
time: 289 us; the launch traced here: 288 us
  waiting for transfers between devices  78.2 us (27%)
  matrix products  68.5 us (24%)
  blocking collectives  59.8 us (21%)
  other arithmetic  26.5 us (9%)
  local copies, waits for them, and re-layouts  24.9 us (9%)
  starting transfers between devices  16.3 us (6%)
  between operations  13.7 us (5%)
    all_to_all x1, waiting for transfers between devices, per_device(): lax.all_to_all(partial_value, 'req', split_axis=0, concat_axis=0, tiled=T...  47.1 us
    all_to_all x1, blocking collectives, per_device(): lax.all_to_all(buffer, 'exp', split_axis=0, concat_axis=0, tiled=True)  30.3 us
    all_to_all x1, blocking collectives, per_device(): lax.all_to_all(expert_out.astype(jnp.bfloat16).reshape(EXPERTS, slots, re...  29.5 us
    dot_general x8, matrix products, per_block(): jnp.einsum('hqgk,gkhd->qhd', exp_terms.astype(jnp.bfloat16), val_grid, pr...  22 us
    dot_general x8, matrix products, per_block(): jnp.einsum('qhd,gkhd->hqgk', query_grid, key_grid, preferred_element_type...  19.1 us
    all_gather x1, waiting for transfers between devices, per_device(): lax.all_gather(queries, 'req', axis=0, tiled=True)  16.6 us
    unnamed x21, local copies, waits for them, and re-layouts  14.2 us
    reduce_sum x8, other arithmetic, per_block(): totals = jnp.sum(exp_terms, axis=(2, 3))  13.7 us
  transfers between devices with their start and end apart: 5, of which 4 were waited for; matrix products, arithmetic and copies ran while one was open for 33% of the time, Pallas kernels for 0%

profile of v1, /device:TPU:0, one launch (start us, length us, event | category | flops | bytes accessed | tf_op | source)
XLA Modules:
  0.0 288.0 jit_solution(17721634932841118999)
XLA Ops:
  10.2 4.4 %all-to-all-start = ((s32[8,1,1024]{2,1,0:T(1,128)}), s32[8,1,1024]{2,1,0:T(1,128)S(1)}, u32[]{:S(2)}, u32[]{:S(2)}) async-start(s32[8,1,1024]{2,1,0:T(1,128)} %stack.3), calls=%async_computation | async-start | bytes 65536 | tf_op jit(solution)/shard_map/all_to_all | solution.py:174
  15.4 4.7 %all-to-all-done = s32[8,1,1024]{2,1,0:T(1,128)S(1)} async-done(((s32[8,1,1024]{2,1,0:T(1,128)}), s32[8,1,1024]{2,1,0:T(1,128)S(1)}, u32[]{:S(2)}, u32[]{:S(2)}) %all-to-all-start) | async-done | bytes 32800 | tf_op jit(solution)/shard_map/all_to_all | solution.py:174
  20.1 16.6 %all-gather.3.cloned.1.call-done = bf16[8192,128]{1,0:T(8,128)(2,1)} async-done(((bf16[1024,128]{1,0:T(8,128)(2,1)}), bf16[8192,128]{1,0:T(8,128)(2,1)}) %all-gather.3.cloned.1.call-update) | async-done | bytes 2097168 | tf_op jit(solution)/shard_map/all_gather | solution.py:178
  36.7 55.3 %while.2 = (s32[]{:T(128)}, f32[8,1024,128]{1,2,0:T(8,128)}, f32[8,1024,1]{1,2,0:T(1,128)S(1)}, f32[8,1024,1]{1,2,0:T(1,128)S(1)}, s32[8,1024]{1,0:T(8,128)S(1)}...) while((s32[]{:T(128)}, f32[8,1024,128]{1,2,0:T(8,128)}, ...), condition=%wide.region_6.7_spmd, body=%wide.region_3.6_spmd.sunk | while | flops 1096812544 | bytes 29160576 | solution.py:76
  36.7 2.4 fusion.102
  40.9 2.8 fusion.103
  47.8 2.7 fusion.103
  50.5 2.4 fusion.102
  54.7 2.7 fusion.103
  61.6 2.7 fusion.103
  64.3 2.4 fusion.102
  68.5 2.7 fusion.103
  75.4 2.8 fusion.103
  78.2 2.4 fusion.102
  82.3 2.8 fusion.103
  85.1 2.4 fusion.102
  89.2 2.8 fusion.103
  92.0 4.9 %pad_maximum_fusion = f32[8,1024,130]{1,2,0:T(8,128)} fusion(f32[8,1024,1]{1,2,0:T(1,128)S(1)} %get-tuple-element.78, f32[8,1024,1]{1,2,0:T(1,128)S(1)} %get-tuple-element.77, f32[8,1024,128]{1,2,0:T(8,128)} %get-tuple-element.76), kind=kLoop, calls=%fused_computation.27 | loop fusion | flops 2129920 | bytes 8519680 | tf_op jit(solution)/shard_map/concatenate | solution.py:34
  97.0 4.8 %all-to-all-start.1 = ((f32[8,1024,130]{1,2,0:T(8,128)}), f32[8,1024,130]{1,2,0:T(8,128)}, u32[]{:S(2)}, u32[]{:S(2)}) async-start(f32[8,1024,130]{1,2,0:T(8,128)} %pad_maximum_fusion), calls=%async_computation.1 | async-start | bytes 8912896 | tf_op jit(solution)/shard_map/all_to_all | solution.py:184
  107.1 47.1 %all-to-all-done.1 = f32[8,1024,130]{1,2,0:T(8,128)} async-done(((f32[8,1024,130]{1,2,0:T(8,128)}), f32[8,1024,130]{1,2,0:T(8,128)}, u32[]{:S(2)}, u32[]{:S(2)}) %all-to-all-start.1) | async-done | bytes 4259872 | tf_op jit(solution)/shard_map/all_to_all | solution.py:184
  154.2 4.7 %copy.134 = f32[8,1024,130]{1,0,2:T(8,128)S(1)} copy(f32[8,1024,130]{1,2,0:T(8,128)} %all-to-all-done.1) | data formatting | bytes 8519680 | tf_op jit(solution)/shard_map/all_to_all | solution.py:184
  159.3 3.9 %copy.115 = f32[17,8,8,1024]{3,1,2,0:T(8,128)S(1)} copy(f32[17,8,8,1024]{3,2,1,0:T(8,128)S(1)} %bitcast.180) | data formatting | bytes 8912896
  165.8 7.9 %copy.116 = f32[16,8,8,1024]{3,2,1,0:T(8,128)} copy(f32[16,8,8,1024]{3,1,2,0:T(8,128)} %bitcast.184) | data formatting | bytes 8388608
  173.7 3.7 %fusion.26 = f32[1024,128]{0,1:T(8,128)S(1)} fusion(f32[16,8,8,1024]{3,2,1,0:T(8,128)} %copy.116, f32[8,1024]{1,0:T(8,128)S(1)} %subtract_exponential_fusion.2), kind=kLoop, calls=%fused_computation.30 | loop fusion | flops 1966080 | bytes 4751360 | tf_op jit(solution)/shard_map/reduce_sum | solution.py:192
  177.7 3.9 %fusion.68 = bf16[1024,1,128]{2,0,1:T(8,128)(2,1)} fusion(bf16[1024,128]{1,0:T(8,128)(2,1)S(1)} %copy-done.8, f32[1024,1024]{0,1:T(8,128)} %copy-done.1, f32[1024]{0:T(1024)S(1)} %get-tuple-element.109, f32[1024,128]{1,0:T(8,128)S(1)} %copy.91, f32[1024]{0:T(1024)S(1)} %get-tuple-element.101, f32[1024]{0:T(1024)S(1)} %get-tuple-element.103, ...), kind=kOutput, calls=%fused_computation.57 | convolution fusion | flops 271187968 | bytes 5259264 | tf_op jit(solution)/shard_map/while/body/eval_jaxpr/hqk,khd->qhd/dot_general | solution.py:110
  181.7 7.1 %all-to-all-start.2 = ((bf16[16,64,128]{2,1,0:T(8,128)(2,1)}), bf16[16,64,128]{2,1,0:T(8,128)(2,1)S(1)}, u32[]{:S(2)}, u32[]{:S(2)}) async-start(bf16[16,64,128]{2,1,0:T(8,128)(2,1)} %bitcast.22), calls=%async_computation.2 | async-start | bytes 524288 | tf_op jit(solution)/shard_map/all_to_all | solution.py:203
  188.9 8.3 %all-to-all-done.2 = bf16[16,64,128]{2,1,0:T(8,128)(2,1)S(1)} async-done(((bf16[16,64,128]{2,1,0:T(8,128)(2,1)}), bf16[16,64,128]{2,1,0:T(8,128)(2,1)S(1)}, u32[]{:S(2)}, u32[]{:S(2)}) %all-to-all-start.2) | async-done | bytes 262176 | tf_op jit(solution)/shard_map/all_to_all | solution.py:203
  197.2 5.1 %multiply_reduce_fusion = (f32[64]{0:T(128)S(1)}, f32[64,2048]{1,0:T(8,128)S(1)}) fusion(bf16[2048,2048]{1,0:T(8,128)(2,1)} %all-gather.5.cloned.1.call-done, bf16[64,2048]{1,0:T(8,128)(2,1)S(1)} %copy-done.2, bf16[16,64,128]{2,1,0:T(8,128)(2,1)S(1)} %all-to-all-done.2), kind=kOutput, calls=%fused_computation.61 | convolution fusion | flops 537395136 | bytes 9437440 | tf_op jit(solution)/shard_map/dot_general | solution.py:204
  203.1 30.3 %all_to_all.44 = bf16[32,16,2048]{2,1,0:T(8,128)(2,1)S(1)} all-to-all(bf16[32,16,2048]{2,1,0:T(8,128)(2,1)S(1)} %bitcast.186), channel_id=1, replica_groups=mesh['req'=8,'exp'=16] {'exp'}, dimensions={0} | all-to-all | bytes 4194304 | tf_op jit(solution)/shard_map/all_to_all | solution.py:224
  233.4 5.6 %fusion.24 = f32[2,16,16,704]{3,2,1,0:T(8,128)} fusion(bf16[2,2048,704]{1,2,0:T(8,128)(2,1)} %param.29, bf16[16,2,16,2048]{3,2,1,0:T(8,128)(2,1)S(1)} %bitcast.188), kind=kOutput, calls=%fused_computation.25 | convolution fusion | flops 1476395008 | bytes 9306112 | tf_op jit(solution)/shard_map/secd,edf->secf/dot_general | solution.py:227
  239.0 9.7 %fusion.32 = bf16[16,2,16,2048]{3,2,0,1:T(8,128)(2,1)} fusion(bf16[2,704,2048]{2,1,0:T(8,128)(2,1)} %param.31, f32[2,16,16,704]{3,2,1,0:T(8,128)} %fusion.24, bf16[2,2048,704]{1,2,0:T(8,128)(2,1)} %param.30, bf16[16,2,16,2048]{3,2,1,0:T(8,128)(2,1)S(1)} %bitcast.189), kind=kOutput, calls=%fused_computation.37 | convolution fusion | flops 2956001280 | bytes 17170432 | tf_op jit(solution)/shard_map/secf,efd->secd/dot_general | solution.py:230
  250.5 29.5 %all_to_all.45 = bf16[32,16,2048]{2,1,0:T(8,128)(2,1)S(1)} all-to-all(bf16[32,16,2048]{2,1,0:T(8,128)(2,1)S(1)} %bitcast.187), channel_id=1, replica_groups=mesh['req'=8,'exp'=16] {'exp'}, dimensions={0} | all-to-all | bytes 4194304 | tf_op jit(solution)/shard_map/all_to_all | solution.py:231
  (114 shorter events, 37.8 us)
Async XLA Ops:
  6.5 96.9 %copy-start = (bf16[1024,128]{1,0:T(8,128)(2,1)S(1)}, bf16[1024,128]{1,0:T(8,128)(2,1)}, u32[]{:S(2)}) copy-start(bf16[1024,128]{1,0:T(8,128)(2,1)} %param.18) | copy-start | bytes 786436
  6.5 30.2 %all-gather.3.cloned.1.call-start = ((), (), s32[]{:S(2)}) async-start(), calls=%async_computation.5 | async-start | bytes 2359296 | tf_op jit(solution)/shard_map/all_gather | solution.py:178
  10.2 9.8 %all-to-all-start = ((s32[8,1,1024]{2,1,0:T(1,128)}), s32[8,1,1024]{2,1,0:T(1,128)S(1)}, u32[]{:S(2)}, u32[]{:S(2)}) async-start(s32[8,1,1024]{2,1,0:T(1,128)} %stack.3), calls=%async_computation | async-start | bytes 65536 | tf_op jit(solution)/shard_map/all_to_all | solution.py:174
  14.6 182.6 %all-gather.5.cloned.1.call-start = ((), (), s32[]{:S(2)}) async-start(), calls=%async_computation.6 | async-start | bytes 8912896 | tf_op jit(solution)/shard_map/all_gather | solution.py:202
  39.1 1.7 copy-start.7
  46.0 1.7 copy-start.7
  52.9 1.7 copy-start.7
  59.8 1.7 copy-start.7
  66.7 1.7 copy-start.7
  73.6 1.7 copy-start.7
  80.5 1.7 copy-start.7
  87.5 1.7 copy-start.7
  97.0 4.8 %copy-start.4 = (s32[64,4]{0,1:T(4,128)S(1)}, s32[64,4]{0,1:T(4,128)}, u32[]{:S(2)}) copy-start(s32[64,4]{0,1:T(4,128)} %param.27) | copy-start | bytes 3076
  97.0 6.4 %copy-start.6 = (bf16[64,4]{0,1:T(4,128)(2,1)S(1)}, bf16[64,4]{0,1:T(4,128)(2,1)}, u32[]{:S(2)}) copy-start(bf16[64,4]{0,1:T(4,128)(2,1)} %param.28) | copy-start | bytes 1540
  97.0 6.4 %copy-start.5 = (bf16[2048]{0:T(1024)(128)(2,1)S(1)}, bf16[2048]{0:T(1024)(128)(2,1)}, u32[]{:S(2)}) copy-start(bf16[2048]{0:T(1024)(128)(2,1)} %param.26) | copy-start | bytes 12292
  97.0 6.5 %copy-start.3 = (bf16[1024,128]{1,0:T(8,128)(2,1)S(1)}, bf16[1024,128]{1,0:T(8,128)(2,1)}, u32[]{:S(2)}) copy-start(bf16[1024,128]{1,0:T(8,128)(2,1)} %param.17) | copy-start | bytes 786436
  97.0 57.3 %all-to-all-start.1 = ((f32[8,1024,130]{1,2,0:T(8,128)}), f32[8,1024,130]{1,2,0:T(8,128)}, u32[]{:S(2)}, u32[]{:S(2)}) async-start(f32[8,1024,130]{1,2,0:T(8,128)} %pad_maximum_fusion), calls=%async_computation.1 | async-start | bytes 8912896 | tf_op jit(solution)/shard_map/all_to_all | solution.py:184
  104.5 2.0 copy-start.1
  173.7 4.0 %copy-start.8 = (bf16[1024,128]{1,0:T(8,128)(2,1)S(1)}, bf16[1024,128]{1,0:T(8,128)(2,1)}, u32[]{:S(2)}) copy-start(bf16[1024,128]{1,0:T(8,128)(2,1)} %param.19) | copy-start | bytes 786436
  177.4 19.8 %copy-start.2 = (bf16[64,2048]{1,0:T(8,128)(2,1)S(1)}, bf16[64,2048]{1,0:T(8,128)(2,1)}, u32[]{:S(2)}) copy-start(bf16[64,2048]{1,0:T(8,128)(2,1)} %param.24) | copy-start | bytes 786436
  181.7 15.6 %all-to-all-start.2 = ((bf16[16,64,128]{2,1,0:T(8,128)(2,1)}), bf16[16,64,128]{2,1,0:T(8,128)(2,1)S(1)}, u32[]{:S(2)}, u32[]{:S(2)}) async-start(bf16[16,64,128]{2,1,0:T(8,128)(2,1)} %bitcast.22), calls=%async_computation.2 | async-start | bytes 524288 | tf_op jit(solution)/shard_map/all_to_all | solution.py:203
Sparse Core Ops, SparseCore 0:
  9.1 27.5 all-gather.2
  38.8 71.1 all-gather.4
